TPU v7x, 32 devices: a whole 2x2x4 slice. The times are simulated.
32 devices in a mesh: lat: 8 (over y, x, core), lon: 4 (over z).
Axes of the slice: x: 2, y: 2, z: 4, core: 2. Of those that a mesh axis runs over, the one named last changes fastest.
Arguments:
- tracer: float32 [16, 64, 2880], P(None, 'lat', 'lon'), may hold values from -6 to 6
- zonal_courant: float32 [16, 64, 2880], P(None, 'lat', 'lon'), may hold values from -0.35 to 0.35
- north_courant: float32 [16, 64, 2880], P(None, 'lat', 'lon'), may hold values from -0.35 to 0.35
- cutoff: int32 [16], replicated, may hold values from 1 to 128
Outputs:
- advanced: float32 [16, 64, 2880], P(None, 'lat', 'lon')
All inputs are finite; a program needn't handle non-finite values.
Results may differ from a plain program's by a relative error of at most 0.0001.
Values sent between devices are 32-bit elements; how exact they have to be, the bound alone decides.
A program may use at most 64 MiB of HBM per device.

v0:
```python
import math
import jax
import jax.numpy as jnp
from jax import lax
from jax.sharding import PartitionSpec as P

NLON = 2880
KMAX = 128
DIFFUSION = 0.2


def with_halo(block, sides, width, periodic):
    for axis, dim in sides:
        count = lax.axis_size(axis)
        forward = [(i, i + 1) for i in range(count - 1)]
        if periodic:
            forward.append((count - 1, 0))
        backward = [(target, source) for source, target in forward]
        low = lax.ppermute(
            lax.slice_in_dim(block, block.shape[dim] - width, None, axis=dim), axis, forward
        )
        high = lax.ppermute(lax.slice_in_dim(block, 0, width, axis=dim), axis, backward)
        block = jnp.concatenate([low, block, high], axis=dim)
    return block


def shifted(block, axis, distance):
    devices = range(lax.axis_size(axis))
    route = [((i - distance) % len(devices), i) for i in devices]
    return lax.ppermute(block, axis, route)


def fourier_tables(columns):
    modes = jnp.arange(KMAX, dtype=jnp.int32)
    product = columns[:, None] * modes[None, :] % NLON
    phase_angle = product.astype(jnp.float32) * (2.0 * math.pi / NLON)
    weights = jnp.where(modes == 0, 1.0 / NLON, 2.0 / NLON).astype(jnp.float32)
    cosine = jnp.cos(phase_angle)
    sine = jnp.sin(phase_angle)
    analysis = jnp.concatenate([cosine * weights[None, :], sine * weights[None, :]], axis=1)
    synthesis = jnp.concatenate([cosine, sine], axis=1).T
    return (analysis, synthesis)


def mode_mask(cut_values):
    modes = jnp.arange(KMAX, dtype=jnp.float32)
    doubled = jnp.concatenate([modes, modes])
    return (doubled[None, :] < cut_values[:, None]).astype(jnp.float32)


def shards(tracer, zonal_courant, north_courant, cutoff):
    level_count, row_count, col_count = tracer.shape
    lat_count = lax.axis_size("lat")
    lon_count = lax.axis_size("lon")
    lat_at = lax.axis_index("lat")
    lon_at = lax.axis_index("lon")
    cap_blocks = lat_count // 8
    polar = (lat_at < cap_blocks) | (lat_at >= lat_count - cap_blocks)
    offset = jnp.where(
        lat_at < cap_blocks,
        lat_at * row_count,
        jnp.where(polar, (lat_at - lat_count + 2 * cap_blocks) * row_count, 0),
    )
    row_cut = lax.dynamic_slice_in_dim(cutoff, offset, row_count).astype(jnp.float32)
    flat_count = level_count * row_count
    flat_cut = jnp.broadcast_to(row_cut[None, :], (level_count, row_count)).reshape(flat_count)
    local_columns = lon_at * col_count + jnp.arange(col_count, dtype=jnp.int32)
    analysis, synthesis = fourier_tables(local_columns)
    state = tracer
    for substep in range(2):
        padded = with_halo(state, (("lat", 1),), 1, False)
        edge_rows = jnp.concatenate([state[:, :1], state[:, -1:]], axis=1)
        opposite = shifted(edge_rows, "lon", lon_count // 2)
        south_rim = jnp.where(lat_at == 0, opposite[:, 0], padded[:, 0])
        north_rim = jnp.where(lat_at == lat_count - 1, opposite[:, 1], padded[:, -1])
        padded = jnp.concatenate([south_rim[:, None], padded[:, 1:-1], north_rim[:, None]], axis=1)
        padded = with_halo(padded, (("lon", 2),), 1, True)
        center = padded[:, 1:-1, 1:-1]
        east_cell = padded[:, 1:-1, 2:]
        west_cell = padded[:, 1:-1, :-2]
        north_cell = padded[:, 2:, 1:-1]
        south_cell = padded[:, :-2, 1:-1]
        tendency = (
            -0.5 * zonal_courant * (east_cell - west_cell)
            - 0.5 * north_courant * (north_cell - south_cell)
            + DIFFUSION * (east_cell + west_cell + north_cell + south_cell - 4.0 * center)
        )
        flat_rows = tendency.reshape(flat_count, col_count)
        partial_coeffs = jnp.dot(flat_rows, analysis, precision=lax.Precision.HIGHEST)
        coefficients = lax.psum(partial_coeffs, "lon")
        coefficients = coefficients * mode_mask(flat_cut)
        filtered = jnp.dot(coefficients, synthesis, precision=lax.Precision.HIGHEST)
        filtered = filtered.reshape(level_count, row_count, col_count)
        state = state + jnp.where(polar, filtered, tendency)
    return state


def solution(mesh):
    return jax.shard_map(
        shards,
        mesh=mesh,
        in_specs=(P(None, "lat", "lon"), P(None, "lat", "lon"), P(None, "lat", "lon"), P()),
        out_specs=P(None, "lat", "lon"),
        check_vma=False,
    )
```

profile of v0, /device:TPU:0, one launch (start us, length us, event | category | flops | bytes accessed | tf_op | source)
XLA Modules:
  0.0 136.2 jit_solution(5212779486867433260)
XLA Ops:
  6.5 0.0 all-reduce.3.cloned.1.call-start
  6.5 1.2 fusion.28
  7.7 2.4 %collective-permute-start.1 = (f32[16,1,720]{2,1,0:T(1,128)S(1)}, f32[16,1,720]{2,1,0:T(1,128)S(1)}, u32[]{:S(2)}, u32[]{:S(2)}) collective-permute-start(f32[16,1,720]{2,1,0:T(1,128)S(1)} %get-tuple-element.11), channel_id=1, source_target_pairs={{0,4},{4,8},{8,12},{12,16},{16,20},{20,24},{24,28},{1,5},{5,9},{9,... | collective-permute-start | bytes 138248 | tf_op jit(solution)/shard_map/ppermute | solution.py:19
  10.1 1.3 collective-permute-start.2
  11.4 0.1 pad_maximum_fusion.28
  11.5 3.5 %collective-permute-start = (f32[16,2,720]{2,1,0:T(2,128)S(1)}, f32[16,2,720]{2,1,0:T(2,128)S(1)}, u32[]{:S(2)}, u32[]{:S(2)}) collective-permute-start(f32[16,2,720]{2,1,0:T(2,128)S(1)} %pad_maximum_fusion.28), channel_id=1, source_target_pairs={{2,0},{3,1},{0,2},{1,3},{6,4},{7,5},{4,6},{5,7},{10,8},{11,9},{8,1... | collective-permute-start | bytes 276488 | tf_op jit(solution)/shard_map/ppermute | solution.py:30
  15.0 0.0 copy-start
  15.0 1.6 %broadcast_multiply_fusion.1 = (f32[720,128]{1,0:T(8,128)S(1)}, f32[720,128]{1,0:T(8,128)S(1)}, f32[720,128]{1,0:T(8,128)S(1)}, f32[720,128]{1,0:T(8,128)S(1)}) fusion(f32[128]{0:T(128)S(1)} %compare_select_fusion.4, s32[720]{0:T(1024)S(1)} %iota_add_fusion), kind=kLoop, calls=%fused_computation.40 | loop fusion | flops 1013760 | bytes 1477952 | tf_op jit(solution)/shard_map/mul | solution.py:40
  16.7 0.0 collective-permute-done.1
  16.7 0.0 collective-permute-done.2
  16.7 0.9 collective-permute-done
  17.6 0.0 copy-start.2
  17.6 0.1 broadcast_select_fusion.3
  17.7 0.0 copy-start.1
  17.7 0.0 copy-done
  17.8 0.1 pad_maximum_fusion.25
  17.9 3.8 %collective-permute-start.4 = (f32[16,10,1]{2,1,0:T(8,128)S(1)}, f32[16,10,1]{2,1,0:T(8,128)S(1)}, u32[]{:S(2)}, u32[]{:S(2)}) collective-permute-start(f32[16,10,1]{2,1,0:T(8,128)S(1)} %get-tuple-element.7), channel_id=1, source_target_pairs={{0,1},{1,2},{2,3},{3,0},{4,5},{5,6},{6,7},{7,4},{8,9},{9,10},{10,1... | collective-permute-start | bytes 1928 | tf_op jit(solution)/shard_map/ppermute | solution.py:19
  21.7 2.9 %collective-permute-start.3 = (f32[16,10,1]{2,1,0:T(8,128)S(1)}, f32[16,10,1]{2,1,0:T(8,128)}, u32[]{:S(2)}, u32[]{:S(2)}) collective-permute-start(f32[16,10,1]{2,1,0:T(8,128)S(1)} %get-tuple-element.8), channel_id=1, source_target_pairs={{1,0},{2,1},{3,2},{0,3},{5,4},{6,5},{7,6},{4,7},{9,8},{10,9},{11,1... | collective-permute-start | bytes 1928 | tf_op jit(solution)/shard_map/ppermute | solution.py:22
  24.6 4.3 %collective-permute-done.4 = f32[16,10,1]{2,1,0:T(8,128)S(1)} collective-permute-done((f32[16,10,1]{2,1,0:T(8,128)S(1)}, f32[16,10,1]{2,1,0:T(8,128)S(1)}, u32[]{:S(2)}, u32[]{:S(2)}) %collective-permute-start.4) | collective-permute-done | bytes 672 | tf_op jit(solution)/shard_map/ppermute | solution.py:19
  28.9 0.0 copy-start.3
  28.9 0.7 copy-done.3
  29.6 0.7 collective-permute-done.3
  30.3 0.0 copy-done.2
  30.3 0.0 copy-done.1
  30.3 1.6 %multiply_add_fusion.1 = f32[16,8,720]{2,1,0:T(8,128)S(1)} fusion(f32[16,8,720]{2,1,0:T(8,128)S(1)} %copy-done, f32[16,1,720]{2,1,0:T(1,128)S(1)} %get-tuple-element.16, f32[16,1,720]{2,1,0:T(1,128)S(1)} %get-tuple-element.15, f32[16,10,1]{2,1,0:T(8,128)} %collective-permute-done.3, f32[16,10,1]{2,1,0:T(8,128)} %copy-done.3, f32[16,8,720]{2,1,0:T(8,128)S(1)} %copy-done.1, ...), kind=kLoop, calls=%fused_computation.30 | loop fusion | flops 2027520 | bytes 1568000 | tf_op jit(solution)/shard_map/add | solution.py:84
  31.8 1.2 fusion.5
  33.0 0.0 copy-start.4
  33.0 0.0 all-reduce.3.cloned.1.call-update
  33.0 0.0 all-reduce.5.cloned.1.call-start
  33.1 0.6 copy-done.4
  33.7 0.1 dynamic-slice_convert_fusion
  33.7 0.1 lt.38
  33.9 35.7 %all-reduce.3.cloned.1.call-done = f32[128,256]{1,0:T(8,128)} async-done(((f32[128,256]{1,0:T(8,128)}), f32[128,256]{1,0:T(8,128)}) %all-reduce.3.cloned.1.call-update) | async-done | bytes 131088 | tf_op jit(solution)/shard_map/psum | solution.py:90
  69.5 1.7 %fusion.1 = f32[16,8,720]{2,1,0:T(8,128)S(1)} fusion(f32[16,8,720]{2,1,0:T(8,128)S(1)} %copy-done, f32[16,8,720]{2,1,0:T(8,128)S(1)} %multiply_add_fusion.1, f32[720,128]{1,0:T(8,128)S(1)} %get-tuple-element.19, f32[720,128]{1,0:T(8,128)S(1)} %get-tuple-element.20, pred[]{:T(512)S(6)} %or.3, f32[128,256]{1,0:T(8,128)} %all-reduce.3.cloned.1.call-done, ...), kind=kOutput, calls=%fused_computation.3 | convolution fusion | flops 283549696 | bytes 1975809 | tf_op jit(solution)/shard_map/dot_general | solution.py:92
  71.3 0.1 fusion.27
  71.3 0.1 pad_maximum_fusion.29
  71.4 2.1 %collective-permute-start.5 = (f32[16,2,720]{2,1,0:T(2,128)S(1)}, f32[16,2,720]{2,1,0:T(2,128)S(1)}, u32[]{:S(2)}, u32[]{:S(2)}) collective-permute-start(f32[16,2,720]{2,1,0:T(2,128)S(1)} %pad_maximum_fusion.29), channel_id=1, source_target_pairs={{2,0},{3,1},{0,2},{1,3},{6,4},{7,5},{4,6},{5,7},{10,8},{11,9},{8,1... | collective-permute-start | bytes 276488 | tf_op jit(solution)/shard_map/ppermute | solution.py:30
  73.6 1.3 collective-permute-start.6
  74.9 1.3 collective-permute-start.7
  76.2 0.0 collective-permute-done.6
  76.2 3.5 %collective-permute-done.7 = f32[16,1,720]{2,1,0:T(1,128)S(1)} collective-permute-done((f32[16,1,720]{2,1,0:T(1,128)S(1)}, f32[16,1,720]{2,1,0:T(1,128)S(1)}, u32[]{:S(2)}, u32[]{:S(2)}) %collective-permute-start.7) | collective-permute-done | bytes 46112 | tf_op jit(solution)/shard_map/ppermute | solution.py:22
  79.7 0.0 collective-permute-done.5
  79.7 0.1 broadcast_select_fusion.2
  79.8 0.1 pad_maximum_fusion.22
  80.0 0.6 collective-permute-start.9
  80.6 3.3 %collective-permute-start.8 = (f32[16,10,1]{2,1,0:T(8,128)S(1)}, f32[16,10,1]{2,1,0:T(8,128)S(1)}, u32[]{:S(2)}, u32[]{:S(2)}) collective-permute-start(f32[16,10,1]{2,1,0:T(8,128)S(1)} %get-tuple-element.6), channel_id=1, source_target_pairs={{1,0},{2,1},{3,2},{0,3},{5,4},{6,5},{7,6},{4,7},{9,8},{10,9},{11,1... | collective-permute-start | bytes 1928 | tf_op jit(solution)/shard_map/ppermute | solution.py:22
  83.9 3.0 %collective-permute-done.9 = f32[16,10,1]{2,1,0:T(8,128)S(1)} collective-permute-done((f32[16,10,1]{2,1,0:T(8,128)S(1)}, f32[16,10,1]{2,1,0:T(8,128)S(1)}, u32[]{:S(2)}, u32[]{:S(2)}) %collective-permute-start.9) | collective-permute-done | bytes 672 | tf_op jit(solution)/shard_map/ppermute | solution.py:19
  86.9 0.1 collective-permute-done.8
  87.0 0.6 multiply_add_fusion
  87.7 1.2 fusion.4
  88.8 0.0 all-reduce.5.cloned.1.call-update
  88.9 38.0 %all-reduce.5.cloned.1.call-done = f32[128,256]{1,0:T(8,128)} async-done(((f32[128,256]{1,0:T(8,128)}), f32[128,256]{1,0:T(8,128)}) %all-reduce.5.cloned.1.call-update) | async-done | bytes 131088 | tf_op jit(solution)/shard_map/psum | solution.py:90
  126.9 2.5 %fusion.3 = f32[16,8,720]{2,1,0:T(8,128)} fusion(f32[16,8,720]{2,1,0:T(8,128)S(1)} %fusion.1, f32[16,8,720]{2,1,0:T(8,128)S(1)} %multiply_add_fusion, f32[720,128]{1,0:T(8,128)S(1)} %get-tuple-element.19, f32[720,128]{1,0:T(8,128)S(1)} %get-tuple-element.20, pred[]{:T(512)S(6)} %or.3, f32[128,256]{1,0:T(8,128)} %all-reduce.5.cloned.1.call-done, ...), kind=kOutput, calls=%fused_computation.5 | convolution fusion | flops 283549696 | bytes 1975809 | tf_op jit(solution)/shard_map/dot_general | solution.py:92
  (5 shorter events, 0.0 us)
Async XLA Ops:
  6.5 63.0 %all-reduce.3.cloned.1.call-start = ((), (), s32[]{:S(2)}) async-start(), calls=%async_computation | async-start | bytes 262144 | tf_op jit(solution)/shard_map/psum | solution.py:90
  7.7 8.9 %collective-permute-start.1 = (f32[16,1,720]{2,1,0:T(1,128)S(1)}, f32[16,1,720]{2,1,0:T(1,128)S(1)}, u32[]{:S(2)}, u32[]{:S(2)}) collective-permute-start(f32[16,1,720]{2,1,0:T(1,128)S(1)} %get-tuple-element.11), channel_id=1, source_target_pairs={{0,4},{4,8},{8,12},{12,16},{16,20},{20,24},{24,28},{1,5},{5,9},{9,... | collective-permute-start | bytes 138248 | tf_op jit(solution)/shard_map/ppermute | solution.py:19
  10.1 6.5 %collective-permute-start.2 = (f32[16,1,720]{2,1,0:T(1,128)S(1)}, f32[16,1,720]{2,1,0:T(1,128)S(1)}, u32[]{:S(2)}, u32[]{:S(2)}) collective-permute-start(f32[16,1,720]{2,1,0:T(1,128)S(1)} %get-tuple-element.12), channel_id=1, source_target_pairs={{4,0},{8,4},{12,8},{16,12},{20,16},{24,20},{28,24},{5,1},{9,5},{13... | collective-permute-start | bytes 138248 | tf_op jit(solution)/shard_map/ppermute | solution.py:22
  11.5 6.1 %collective-permute-start = (f32[16,2,720]{2,1,0:T(2,128)S(1)}, f32[16,2,720]{2,1,0:T(2,128)S(1)}, u32[]{:S(2)}, u32[]{:S(2)}) collective-permute-start(f32[16,2,720]{2,1,0:T(2,128)S(1)} %pad_maximum_fusion.28), channel_id=1, source_target_pairs={{2,0},{3,1},{0,2},{1,3},{6,4},{7,5},{4,6},{5,7},{10,8},{11,9},{8,1... | collective-permute-start | bytes 276488 | tf_op jit(solution)/shard_map/ppermute | solution.py:30
  15.0 2.7 %copy-start = (f32[16,8,720]{2,1,0:T(8,128)S(1)}, f32[16,8,720]{2,1,0:T(8,128)}, u32[]{:S(2)}) copy-start(f32[16,8,720]{2,1,0:T(8,128)} %param.4) | copy-start | bytes 1105924
  17.6 12.7 %copy-start.2 = (f32[16,8,720]{2,1,0:T(8,128)S(1)}, f32[16,8,720]{2,1,0:T(8,128)}, u32[]{:S(2)}) copy-start(f32[16,8,720]{2,1,0:T(8,128)} %param.5) | copy-start | bytes 1105924
  17.7 12.5 %copy-start.1 = (f32[16,8,720]{2,1,0:T(8,128)S(1)}, f32[16,8,720]{2,1,0:T(8,128)}, u32[]{:S(2)}) copy-start(f32[16,8,720]{2,1,0:T(8,128)} %param.6) | copy-start | bytes 1105924
  17.9 11.0 %collective-permute-start.4 = (f32[16,10,1]{2,1,0:T(8,128)S(1)}, f32[16,10,1]{2,1,0:T(8,128)S(1)}, u32[]{:S(2)}, u32[]{:S(2)}) collective-permute-start(f32[16,10,1]{2,1,0:T(8,128)S(1)} %get-tuple-element.7), channel_id=1, source_target_pairs={{0,1},{1,2},{2,3},{3,0},{4,5},{5,6},{6,7},{7,4},{8,9},{9,10},{10,1... | collective-permute-start | bytes 1928 | tf_op jit(solution)/shard_map/ppermute | solution.py:19
  21.7 8.5 %collective-permute-start.3 = (f32[16,10,1]{2,1,0:T(8,128)S(1)}, f32[16,10,1]{2,1,0:T(8,128)}, u32[]{:S(2)}, u32[]{:S(2)}) collective-permute-start(f32[16,10,1]{2,1,0:T(8,128)S(1)} %get-tuple-element.8), channel_id=1, source_target_pairs={{1,0},{2,1},{3,2},{0,3},{5,4},{6,5},{7,6},{4,7},{9,8},{10,9},{11,1... | collective-permute-start | bytes 1928 | tf_op jit(solution)/shard_map/ppermute | solution.py:22
  28.9 0.7 copy-start.3
  33.0 0.7 copy-start.4
  33.0 93.9 %all-reduce.5.cloned.1.call-start = ((), (), s32[]{:S(2)}) async-start(), calls=%async_computation.1 | async-start | bytes 262144 | tf_op jit(solution)/shard_map/psum | solution.py:90
  71.4 8.3 %collective-permute-start.5 = (f32[16,2,720]{2,1,0:T(2,128)S(1)}, f32[16,2,720]{2,1,0:T(2,128)S(1)}, u32[]{:S(2)}, u32[]{:S(2)}) collective-permute-start(f32[16,2,720]{2,1,0:T(2,128)S(1)} %pad_maximum_fusion.29), channel_id=1, source_target_pairs={{2,0},{3,1},{0,2},{1,3},{6,4},{7,5},{4,6},{5,7},{10,8},{11,9},{8,1... | collective-permute-start | bytes 276488 | tf_op jit(solution)/shard_map/ppermute | solution.py:30
  73.6 2.6 %collective-permute-start.6 = (f32[16,1,720]{2,1,0:T(1,128)S(1)}, f32[16,1,720]{2,1,0:T(1,128)S(1)}, u32[]{:S(2)}, u32[]{:S(2)}) collective-permute-start(f32[16,1,720]{2,1,0:T(1,128)S(1)} %get-tuple-element.9), channel_id=1, source_target_pairs={{0,4},{4,8},{8,12},{12,16},{16,20},{20,24},{24,28},{1,5},{5,9},{9,... | collective-permute-start | bytes 138248 | tf_op jit(solution)/shard_map/ppermute | solution.py:19
  74.9 4.9 %collective-permute-start.7 = (f32[16,1,720]{2,1,0:T(1,128)S(1)}, f32[16,1,720]{2,1,0:T(1,128)S(1)}, u32[]{:S(2)}, u32[]{:S(2)}) collective-permute-start(f32[16,1,720]{2,1,0:T(1,128)S(1)} %get-tuple-element.10), channel_id=1, source_target_pairs={{4,0},{8,4},{12,8},{16,12},{20,16},{24,20},{28,24},{5,1},{9,5},{13... | collective-permute-start | bytes 138248 | tf_op jit(solution)/shard_map/ppermute | solution.py:22
  80.0 6.9 %collective-permute-start.9 = (f32[16,10,1]{2,1,0:T(8,128)S(1)}, f32[16,10,1]{2,1,0:T(8,128)S(1)}, u32[]{:S(2)}, u32[]{:S(2)}) collective-permute-start(f32[16,10,1]{2,1,0:T(8,128)S(1)} %get-tuple-element.5), channel_id=1, source_target_pairs={{0,1},{1,2},{2,3},{3,0},{4,5},{5,6},{6,7},{7,4},{8,9},{9,10},{10,1... | collective-permute-start | bytes 1928 | tf_op jit(solution)/shard_map/ppermute | solution.py:19
  80.6 6.4 %collective-permute-start.8 = (f32[16,10,1]{2,1,0:T(8,128)S(1)}, f32[16,10,1]{2,1,0:T(8,128)S(1)}, u32[]{:S(2)}, u32[]{:S(2)}) collective-permute-start(f32[16,10,1]{2,1,0:T(8,128)S(1)} %get-tuple-element.6), channel_id=1, source_target_pairs={{1,0},{2,1},{3,2},{0,3},{5,4},{6,5},{7,6},{4,7},{9,8},{10,9},{11,1... | collective-permute-start | bytes 1928 | tf_op jit(solution)/shard_map/ppermute | solution.py:22
Sparse Core Ops, SparseCore 0:
  33.1 36.3 all-reduce.2
  89.0 37.8 all-reduce.4
where the time goes:
time: 136 us
  waiting for transfers between devices  86.4 us (64%)
  starting transfers between devices  22.5 us (17%)
  between operations  13.6 us (10%)
  matrix products  6.6 us (5%)
  other arithmetic  4.59 us (3%)
  local copies, waits for them, and re-layouts  2.6 us (2%)
    psum x2, waiting for transfers between devices, shards(): coefficients = lax.psum(partial_coeffs, 'lon')  73.7 us
    ppermute x4, starting transfers between devices, with_halo(): lax.ppermute(lax.slice_in_dim(block, 0, width, axis=dim), axis, backward)  8.73 us
    ppermute x4, starting transfers between devices, with_halo(): lax.ppermute(lax.slice_in_dim(block, block.shape[dim] - width, None, axis...  8.12 us
    ppermute x4, waiting for transfers between devices, with_halo(): lax.ppermute(lax.slice_in_dim(block, block.shape[dim] - width, None, axis...  7.37 us
    ppermute x2, starting transfers between devices, shifted(): return lax.ppermute(block, axis, route)  5.61 us
    ppermute x4, waiting for transfers between devices, with_halo(): lax.ppermute(lax.slice_in_dim(block, 0, width, axis=dim), axis, backward)  4.34 us
    dot_general x2, matrix products, shards(): filtered = jnp.dot(coefficients, synthesis, precision=lax.Precision.HIGHEST)  4.25 us
  transfers between devices with their start and end apart: 12, of which 8 were waited for; matrix products, arithmetic and copies ran while one was open for 1% of the time, Pallas kernels for 0%

commit v1 on v0

--- a/solution.py
+++ b/solution.py
@@ -87,7 +87,7 @@
         )
         flat_rows = tendency.reshape(flat_count, col_count)
         partial_coeffs = jnp.dot(flat_rows, analysis, precision=lax.Precision.HIGHEST)
-        coefficients = lax.psum(partial_coeffs, "lon")
+        coefficients = jnp.sum(lax.all_gather(partial_coeffs, "lon"), axis=0)
         coefficients = coefficients * mode_mask(flat_cut)
         filtered = jnp.dot(coefficients, synthesis, precision=lax.Precision.HIGHEST)
         filtered = filtered.reshape(level_count, row_count, col_count)

time: 136 us -> 79.9 us (0.59)
  waiting for transfers between devices: 86.4 us -> 17.9 us
  blocking collectives: 0 us -> 31 us
  between operations: 13.6 us -> 0.22 us
  matrix products: 6.6 us -> 3.48 us
    psum x2 -> x0, waiting for transfers between devices: 73.7 us -> none  [shards(): coefficients = lax.psum(partial_coeffs, 'lon')]
    all_gather x0 -> x2, blocking collectives: none -> 31 us  [shards(): coefficients = jnp.sum(lax.all_gather(partial_coeffs, 'lon'), axis=0)]
    ppermute x4, waiting for transfers between devices: 4.34 us -> 9.99 us  [with_halo(): lax.ppermute(lax.slice_in_dim(block, 0, width, axis=dim), axis, backward)]
    ppermute x4, starting transfers between devices: 8.12 us -> 11.5 us  [with_halo(): lax.ppermute(lax.slice_in_dim(block, block.shape[dim] - width, None, axis...]
    ppermute x4, starting transfers between devices: 8.73 us -> 5.47 us  [with_halo(): lax.ppermute(lax.slice_in_dim(block, 0, width, axis=dim), axis, backward)]
    dot_general x2, matrix products: 4.25 us -> 2.44 us  [shards(): filtered = jnp.dot(coefficients, synthesis, precision=lax.Precision.HIGHEST)]
    ppermute x2, starting transfers between devices: 5.61 us -> 4.23 us  [shifted(): return lax.ppermute(block, axis, route)]
  transfers between devices with their start and end apart: 12 -> 10, of which waited for: 8 -> 6; matrix products, arithmetic and copies ran while one was open for 1% -> 2% of each run, Pallas kernels for 0% -> 0%
where the time goes in v1:
time: 79.9 us; the launch traced here: 78.8 us
  blocking collectives  31 us (39%)
  starting transfers between devices  21.2 us (27%)
  waiting for transfers between devices  17.9 us (22%)
  other arithmetic  3.7 us (5%)
  matrix products  3.48 us (4%)
  local copies, waits for them, and re-layouts  1.37 us (2%)
    all_gather x2, blocking collectives, shards(): coefficients = jnp.sum(lax.all_gather(partial_coeffs, 'lon'), axis=0)  31 us
    ppermute x4, starting transfers between devices, with_halo(): lax.ppermute(lax.slice_in_dim(block, block.shape[dim] - width, None, axis...  11.5 us
    ppermute x4, waiting for transfers between devices, with_halo(): lax.ppermute(lax.slice_in_dim(block, 0, width, axis=dim), axis, backward)  9.99 us
    ppermute x4, waiting for transfers between devices, with_halo(): lax.ppermute(lax.slice_in_dim(block, block.shape[dim] - width, None, axis...  7.02 us
    ppermute x4, starting transfers between devices, with_halo(): lax.ppermute(lax.slice_in_dim(block, 0, width, axis=dim), axis, backward)  5.47 us
    ppermute x2, starting transfers between devices, shifted(): return lax.ppermute(block, axis, route)  4.23 us
    dot_general x2, matrix products, shards(): filtered = jnp.dot(coefficients, synthesis, precision=lax.Precision.HIGHEST)  2.44 us
    mul x1, other arithmetic, fourier_tables(): cosine * weights[None, :]  1.62 us
  transfers between devices with their start and end apart: 10, of which 6 were waited for; matrix products, arithmetic and copies ran while one was open for 2% of the time, Pallas kernels for 0%

profile of v1, /device:TPU:0, one launch (start us, length us, event | category | flops | bytes accessed | tf_op | source)
XLA Modules:
  0.0 78.8 jit_solution(9373427743884090129)
XLA Ops:
  0.0 1.2 %fusion.28 = (f32[16,1,720]{2,1,0:T(1,128)S(1)}, f32[16,1,720]{2,1,0:T(1,128)S(1)}) fusion(f32[16,8,720]{2,1,0:T(8,128)} %param.4), kind=kLoop, calls=%fused_computation.72 | loop fusion | bytes 184320 | tf_op jit(solution)/shard_map/slice | solution.py:72
  1.2 2.4 %collective-permute-start.1 = (f32[16,1,720]{2,1,0:T(1,128)S(1)}, f32[16,1,720]{2,1,0:T(1,128)S(1)}, u32[]{:S(2)}, u32[]{:S(2)}) collective-permute-start(f32[16,1,720]{2,1,0:T(1,128)S(1)} %get-tuple-element.11), channel_id=1, source_target_pairs={{0,4},{4,8},{8,12},{12,16},{16,20},{20,24},{24,28},{1,5},{5,9},{9,... | collective-permute-start | bytes 138248 | tf_op jit(solution)/shard_map/ppermute | solution.py:19
  3.6 1.3 %collective-permute-start.2 = (f32[16,1,720]{2,1,0:T(1,128)S(1)}, f32[16,1,720]{2,1,0:T(1,128)S(1)}, u32[]{:S(2)}, u32[]{:S(2)}) collective-permute-start(f32[16,1,720]{2,1,0:T(1,128)S(1)} %get-tuple-element.12), channel_id=1, source_target_pairs={{4,0},{8,4},{12,8},{16,12},{20,16},{24,20},{28,24},{5,1},{9,5},{13... | collective-permute-start | bytes 138248 | tf_op jit(solution)/shard_map/ppermute | solution.py:22
  4.9 0.1 pad_maximum_fusion.28
  5.0 3.5 %collective-permute-start = (f32[16,2,720]{2,1,0:T(2,128)S(1)}, f32[16,2,720]{2,1,0:T(2,128)S(1)}, u32[]{:S(2)}, u32[]{:S(2)}) collective-permute-start(f32[16,2,720]{2,1,0:T(2,128)S(1)} %pad_maximum_fusion.28), channel_id=1, source_target_pairs={{2,0},{3,1},{0,2},{1,3},{6,4},{7,5},{4,6},{5,7},{10,8},{11,9},{8,1... | collective-permute-start | bytes 276488 | tf_op jit(solution)/shard_map/ppermute | solution.py:30
  8.5 0.0 copy-start
  8.5 1.6 %broadcast_multiply_fusion.1 = (f32[720,128]{1,0:T(8,128)S(1)}, f32[720,128]{1,0:T(8,128)S(1)}, f32[720,128]{1,0:T(8,128)S(1)}, f32[720,128]{1,0:T(8,128)S(1)}) fusion(f32[128]{0:T(128)S(1)} %compare_select_fusion.4, s32[720]{0:T(1024)S(1)} %iota_add_fusion), kind=kLoop, calls=%fused_computation.40 | loop fusion | flops 1013760 | bytes 1477952 | tf_op jit(solution)/shard_map/mul | solution.py:40
  10.2 0.0 collective-permute-done.1
  10.2 0.0 collective-permute-done.2
  10.2 0.9 %collective-permute-done = f32[16,2,720]{2,1,0:T(2,128)S(1)} collective-permute-done((f32[16,2,720]{2,1,0:T(2,128)S(1)}, f32[16,2,720]{2,1,0:T(2,128)S(1)}, u32[]{:S(2)}, u32[]{:S(2)}) %collective-permute-start) | collective-permute-done | bytes 92192 | tf_op jit(solution)/shard_map/ppermute | solution.py:30
  11.1 0.0 copy-start.3
  11.1 0.1 broadcast_select_fusion.3
  11.2 0.0 copy-start.1
  11.2 0.0 copy-done
  11.2 0.1 pad_maximum_fusion.25
  11.4 0.0 copy-start.5
  11.4 3.8 %collective-permute-start.4 = (f32[16,10,1]{2,1,0:T(8,128)S(1)}, f32[16,10,1]{2,1,0:T(8,128)S(1)}, u32[]{:S(2)}, u32[]{:S(2)}) collective-permute-start(f32[16,10,1]{2,1,0:T(8,128)S(1)} %get-tuple-element.7), channel_id=1, source_target_pairs={{0,1},{1,2},{2,3},{3,0},{4,5},{5,6},{6,7},{7,4},{8,9},{9,10},{10,1... | collective-permute-start | bytes 1928 | tf_op jit(solution)/shard_map/ppermute | solution.py:19
  15.2 2.9 %collective-permute-start.3 = (f32[16,10,1]{2,1,0:T(8,128)S(1)}, f32[16,10,1]{2,1,0:T(8,128)S(1)}, u32[]{:S(2)}, u32[]{:S(2)}) collective-permute-start(f32[16,10,1]{2,1,0:T(8,128)S(1)} %get-tuple-element.8), channel_id=1, source_target_pairs={{1,0},{2,1},{3,2},{0,3},{5,4},{6,5},{7,6},{4,7},{9,8},{10,9},{11,1... | collective-permute-start | bytes 1928 | tf_op jit(solution)/shard_map/ppermute | solution.py:22
  18.1 0.0 copy-done.5
  18.1 0.1 dynamic-slice_convert_fusion
  18.2 0.1 lt.38
  18.2 4.2 %collective-permute-done.4 = f32[16,10,1]{2,1,0:T(8,128)S(1)} collective-permute-done((f32[16,10,1]{2,1,0:T(8,128)S(1)}, f32[16,10,1]{2,1,0:T(8,128)S(1)}, u32[]{:S(2)}, u32[]{:S(2)}) %collective-permute-start.4) | collective-permute-done | bytes 672 | tf_op jit(solution)/shard_map/ppermute | solution.py:19
  22.4 1.2 %collective-permute-done.3 = f32[16,10,1]{2,1,0:T(8,128)S(1)} collective-permute-done((f32[16,10,1]{2,1,0:T(8,128)S(1)}, f32[16,10,1]{2,1,0:T(8,128)S(1)}, u32[]{:S(2)}, u32[]{:S(2)}) %collective-permute-start.3) | collective-permute-done | bytes 672 | tf_op jit(solution)/shard_map/ppermute | solution.py:22
  23.6 0.0 copy-done.3
  23.6 0.0 copy-done.1
  23.6 0.6 multiply_add_fusion.1
  24.2 0.5 fusion.5
  24.7 15.3 %all-gather = f32[512,256]{1,0:T(8,128)S(1)} all-gather(f32[128,256]{1,0:T(8,128)S(1)} %fusion.5), channel_id=2, replica_groups=mesh['lat'=8,'lon'=4] {'lon'}, dimensions={0}, use_global_device_ids=true | all-gather | bytes 655360 | tf_op jit(solution)/shard_map/all_gather | solution.py:90
  40.1 0.8 %fusion.1 = f32[16,8,720]{2,1,0:T(8,128)S(1)} fusion(f32[16,8,720]{2,1,0:T(8,128)S(1)} %copy-done, f32[16,8,720]{2,1,0:T(8,128)S(1)} %multiply_add_fusion.1, f32[720,128]{1,0:T(8,128)S(1)} %get-tuple-element.19, f32[720,128]{1,0:T(8,128)S(1)} %get-tuple-element.20, pred[]{:T(512)S(6)} %or.3, f32[128,256]{1,0:T(8,128)S(1)} %reduce_sum.18, ...), kind=kOutput, calls=%fused_computation.3 | convolution fusion | flops 283549696 | bytes 1975809 | tf_op jit(solution)/shard_map/dot_general | solution.py:92
  40.9 0.1 fusion.27
  41.0 0.1 pad_maximum_fusion.29
  41.1 0.8 collective-permute-start.5
  41.8 1.3 %collective-permute-start.6 = (f32[16,1,720]{2,1,0:T(1,128)S(1)}, f32[16,1,720]{2,1,0:T(1,128)S(1)}, u32[]{:S(2)}, u32[]{:S(2)}) collective-permute-start(f32[16,1,720]{2,1,0:T(1,128)S(1)} %get-tuple-element.9), channel_id=1, source_target_pairs={{0,4},{4,8},{8,12},{12,16},{16,20},{20,24},{24,28},{1,5},{5,9},{9,... | collective-permute-start | bytes 138248 | tf_op jit(solution)/shard_map/ppermute | solution.py:19
  43.1 1.3 %collective-permute-start.7 = (f32[16,1,720]{2,1,0:T(1,128)S(1)}, f32[16,1,720]{2,1,0:T(1,128)S(1)}, u32[]{:S(2)}, u32[]{:S(2)}) collective-permute-start(f32[16,1,720]{2,1,0:T(1,128)S(1)} %get-tuple-element.10), channel_id=1, source_target_pairs={{4,0},{8,4},{12,8},{16,12},{20,16},{24,20},{28,24},{5,1},{9,5},{13... | collective-permute-start | bytes 138248 | tf_op jit(solution)/shard_map/ppermute | solution.py:22
  44.4 0.0 collective-permute-done.6
  44.4 4.8 %collective-permute-done.7 = f32[16,1,720]{2,1,0:T(1,128)S(1)} collective-permute-done((f32[16,1,720]{2,1,0:T(1,128)S(1)}, f32[16,1,720]{2,1,0:T(1,128)S(1)}, u32[]{:S(2)}, u32[]{:S(2)}) %collective-permute-start.7) | collective-permute-done | bytes 46112 | tf_op jit(solution)/shard_map/ppermute | solution.py:22
  49.2 0.0 collective-permute-done.5
  49.2 0.0 copy-start.4
  49.2 0.1 broadcast_select_fusion.2
  49.3 0.0 copy-start.2
  49.4 0.1 pad_maximum_fusion.22
  49.5 4.0 %collective-permute-start.9 = (f32[16,10,1]{2,1,0:T(8,128)S(1)}, f32[16,10,1]{2,1,0:T(8,128)S(1)}, u32[]{:S(2)}, u32[]{:S(2)}) collective-permute-start(f32[16,10,1]{2,1,0:T(8,128)S(1)} %get-tuple-element.5), channel_id=1, source_target_pairs={{0,1},{1,2},{2,3},{3,0},{4,5},{5,6},{6,7},{7,4},{8,9},{9,10},{10,1... | collective-permute-start | bytes 1928 | tf_op jit(solution)/shard_map/ppermute | solution.py:19
  53.4 0.0 collective-permute-start.8
  53.5 2.9 %collective-permute-done.9 = f32[16,10,1]{2,1,0:T(8,128)S(1)} collective-permute-done((f32[16,10,1]{2,1,0:T(8,128)S(1)}, f32[16,10,1]{2,1,0:T(8,128)S(1)}, u32[]{:S(2)}, u32[]{:S(2)}) %collective-permute-start.9) | collective-permute-done | bytes 672 | tf_op jit(solution)/shard_map/ppermute | solution.py:19
  56.3 4.0 %collective-permute-done.8 = f32[16,10,1]{2,1,0:T(8,128)S(1)} collective-permute-done((f32[16,10,1]{2,1,0:T(8,128)S(1)}, f32[16,10,1]{2,1,0:T(8,128)S(1)}, u32[]{:S(2)}, u32[]{:S(2)}) %collective-permute-start.8) | collective-permute-done | bytes 672 | tf_op jit(solution)/shard_map/ppermute | solution.py:22
  60.3 0.0 copy-done.4
  60.3 0.0 copy-done.2
  60.3 0.6 multiply_add_fusion
  61.0 0.5 fusion.4
  61.5 15.7 %all-gather.1 = f32[512,256]{1,0:T(8,128)S(1)} all-gather(f32[128,256]{1,0:T(8,128)S(1)} %fusion.4), channel_id=3, replica_groups=mesh['lat'=8,'lon'=4] {'lon'}, dimensions={0}, use_global_device_ids=true | all-gather | bytes 655360 | tf_op jit(solution)/shard_map/all_gather | solution.py:90
  77.2 1.6 %fusion.3 = f32[16,8,720]{2,1,0:T(8,128)} fusion(f32[16,8,720]{2,1,0:T(8,128)S(1)} %fusion.1, f32[16,8,720]{2,1,0:T(8,128)S(1)} %multiply_add_fusion, f32[720,128]{1,0:T(8,128)S(1)} %get-tuple-element.19, f32[720,128]{1,0:T(8,128)S(1)} %get-tuple-element.20, pred[]{:T(512)S(6)} %or.3, f32[128,256]{1,0:T(8,128)S(1)} %reduce_sum.19, ...), kind=kOutput, calls=%fused_computation.5 | convolution fusion | flops 283549696 | bytes 1975809 | tf_op jit(solution)/shard_map/dot_general | solution.py:92
  (7 shorter events, 0.1 us)
Async XLA Ops:
  1.2 9.0 %collective-permute-start.1 = (f32[16,1,720]{2,1,0:T(1,128)S(1)}, f32[16,1,720]{2,1,0:T(1,128)S(1)}, u32[]{:S(2)}, u32[]{:S(2)}) collective-permute-start(f32[16,1,720]{2,1,0:T(1,128)S(1)} %get-tuple-element.11), channel_id=1, source_target_pairs={{0,4},{4,8},{8,12},{12,16},{16,20},{20,24},{24,28},{1,5},{5,9},{9,... | collective-permute-start | bytes 138248 | tf_op jit(solution)/shard_map/ppermute | solution.py:19
  3.6 6.6 %collective-permute-start.2 = (f32[16,1,720]{2,1,0:T(1,128)S(1)}, f32[16,1,720]{2,1,0:T(1,128)S(1)}, u32[]{:S(2)}, u32[]{:S(2)}) collective-permute-start(f32[16,1,720]{2,1,0:T(1,128)S(1)} %get-tuple-element.12), channel_id=1, source_target_pairs={{4,0},{8,4},{12,8},{16,12},{20,16},{24,20},{28,24},{5,1},{9,5},{13... | collective-permute-start | bytes 138248 | tf_op jit(solution)/shard_map/ppermute | solution.py:22
  5.0 6.1 %collective-permute-start = (f32[16,2,720]{2,1,0:T(2,128)S(1)}, f32[16,2,720]{2,1,0:T(2,128)S(1)}, u32[]{:S(2)}, u32[]{:S(2)}) collective-permute-start(f32[16,2,720]{2,1,0:T(2,128)S(1)} %pad_maximum_fusion.28), channel_id=1, source_target_pairs={{2,0},{3,1},{0,2},{1,3},{6,4},{7,5},{4,6},{5,7},{10,8},{11,9},{8,1... | collective-permute-start | bytes 276488 | tf_op jit(solution)/shard_map/ppermute | solution.py:30
  8.5 2.7 %copy-start = (f32[16,8,720]{2,1,0:T(8,128)S(1)}, f32[16,8,720]{2,1,0:T(8,128)}, u32[]{:S(2)}) copy-start(f32[16,8,720]{2,1,0:T(8,128)} %param.4) | copy-start | bytes 1105924
  11.1 12.6 %copy-start.3 = (f32[16,8,720]{2,1,0:T(8,128)S(1)}, f32[16,8,720]{2,1,0:T(8,128)}, u32[]{:S(2)}) copy-start(f32[16,8,720]{2,1,0:T(8,128)} %param.5) | copy-start | bytes 1105924
  11.2 12.4 %copy-start.1 = (f32[16,8,720]{2,1,0:T(8,128)S(1)}, f32[16,8,720]{2,1,0:T(8,128)}, u32[]{:S(2)}) copy-start(f32[16,8,720]{2,1,0:T(8,128)} %param.6) | copy-start | bytes 1105924
  11.4 6.7 %copy-start.5 = (s32[16]{0:T(128)S(1)}, s32[16]{0:T(128)}, u32[]{:S(2)}) copy-start(s32[16]{0:T(128)} %param.7) | copy-start | bytes 196
  11.4 11.0 %collective-permute-start.4 = (f32[16,10,1]{2,1,0:T(8,128)S(1)}, f32[16,10,1]{2,1,0:T(8,128)S(1)}, u32[]{:S(2)}, u32[]{:S(2)}) collective-permute-start(f32[16,10,1]{2,1,0:T(8,128)S(1)} %get-tuple-element.7), channel_id=1, source_target_pairs={{0,1},{1,2},{2,3},{3,0},{4,5},{5,6},{6,7},{7,4},{8,9},{9,10},{10,1... | collective-permute-start | bytes 1928 | tf_op jit(solution)/shard_map/ppermute | solution.py:19
  15.2 8.4 %collective-permute-start.3 = (f32[16,10,1]{2,1,0:T(8,128)S(1)}, f32[16,10,1]{2,1,0:T(8,128)S(1)}, u32[]{:S(2)}, u32[]{:S(2)}) collective-permute-start(f32[16,10,1]{2,1,0:T(8,128)S(1)} %get-tuple-element.8), channel_id=1, source_target_pairs={{1,0},{2,1},{3,2},{0,3},{5,4},{6,5},{7,6},{4,7},{9,8},{10,9},{11,1... | collective-permute-start | bytes 1928 | tf_op jit(solution)/shard_map/ppermute | solution.py:22
  41.1 8.1 %collective-permute-start.5 = (f32[16,2,720]{2,1,0:T(2,128)S(1)}, f32[16,2,720]{2,1,0:T(2,128)S(1)}, u32[]{:S(2)}, u32[]{:S(2)}) collective-permute-start(f32[16,2,720]{2,1,0:T(2,128)S(1)} %pad_maximum_fusion.29), channel_id=1, source_target_pairs={{2,0},{3,1},{0,2},{1,3},{6,4},{7,5},{4,6},{5,7},{10,8},{11,9},{8,1... | collective-permute-start | bytes 276488 | tf_op jit(solution)/shard_map/ppermute | solution.py:30
  41.8 2.6 %collective-permute-start.6 = (f32[16,1,720]{2,1,0:T(1,128)S(1)}, f32[16,1,720]{2,1,0:T(1,128)S(1)}, u32[]{:S(2)}, u32[]{:S(2)}) collective-permute-start(f32[16,1,720]{2,1,0:T(1,128)S(1)} %get-tuple-element.9), channel_id=1, source_target_pairs={{0,4},{4,8},{8,12},{12,16},{16,20},{20,24},{24,28},{1,5},{5,9},{9,... | collective-permute-start | bytes 138248 | tf_op jit(solution)/shard_map/ppermute | solution.py:19
  43.1 6.1 %collective-permute-start.7 = (f32[16,1,720]{2,1,0:T(1,128)S(1)}, f32[16,1,720]{2,1,0:T(1,128)S(1)}, u32[]{:S(2)}, u32[]{:S(2)}) collective-permute-start(f32[16,1,720]{2,1,0:T(1,128)S(1)} %get-tuple-element.10), channel_id=1, source_target_pairs={{4,0},{8,4},{12,8},{16,12},{20,16},{24,20},{28,24},{5,1},{9,5},{13... | collective-permute-start | bytes 138248 | tf_op jit(solution)/shard_map/ppermute | solution.py:22
  49.2 11.1 %copy-start.4 = (f32[16,8,720]{2,1,0:T(8,128)S(1)}, f32[16,8,720]{2,1,0:T(8,128)}, u32[]{:S(2)}) copy-start(f32[16,8,720]{2,1,0:T(8,128)} %param.5) | copy-start | bytes 1105924
  49.3 11.0 %copy-start.2 = (f32[16,8,720]{2,1,0:T(8,128)S(1)}, f32[16,8,720]{2,1,0:T(8,128)}, u32[]{:S(2)}) copy-start(f32[16,8,720]{2,1,0:T(8,128)} %param.6) | copy-start | bytes 1105924
  49.5 6.8 %collective-permute-start.9 = (f32[16,10,1]{2,1,0:T(8,128)S(1)}, f32[16,10,1]{2,1,0:T(8,128)S(1)}, u32[]{:S(2)}, u32[]{:S(2)}) collective-permute-start(f32[16,10,1]{2,1,0:T(8,128)S(1)} %get-tuple-element.5), channel_id=1, source_target_pairs={{0,1},{1,2},{2,3},{3,0},{4,5},{5,6},{6,7},{7,4},{8,9},{9,10},{10,1... | collective-permute-start | bytes 1928 | tf_op jit(solution)/shard_map/ppermute | solution.py:19
  53.4 6.9 %collective-permute-start.8 = (f32[16,10,1]{2,1,0:T(8,128)S(1)}, f32[16,10,1]{2,1,0:T(8,128)S(1)}, u32[]{:S(2)}, u32[]{:S(2)}) collective-permute-start(f32[16,10,1]{2,1,0:T(8,128)S(1)} %get-tuple-element.6), channel_id=1, source_target_pairs={{1,0},{2,1},{3,2},{0,3},{5,4},{6,5},{7,6},{4,7},{9,8},{10,9},{11,1... | collective-permute-start | bytes 1928 | tf_op jit(solution)/shard_map/ppermute | solution.py:22
